TPU v7x, 32 devices: a whole 2x2x4 slice. The times are simulated.
32 devices in a mesh: groups: 2 (over x), depth: 8 (over z, y), height: 2 (over core).
Axes of the slice: x: 2, y: 2, z: 4, core: 2. Of those that a mesh axis runs over, the one named last changes fastest.
Arguments:
- images: bfloat16 [4, 4, 64, 16, 256], P('groups', None, 'depth', 'height'), parts along dimension 0, may hold values from -6 to 6
- pre_hidden: bfloat16 [4, 16, 64, 16, 256], P('groups', None, 'depth', 'height'), parts along dimension 0, may hold values from -6 to 6
- pre_deep: bfloat16 [4, 32, 32, 8, 128], P(('groups', 'height'), None, 'depth'), parts along dimension 0, may hold values from -6 to 6
- pooled_grad: bfloat16 [4, 32, 16, 256], P(('groups', 'height'), None, 'depth'), parts along dimension 0, may hold values from -1.25 to 1.25
- deep_weight: bfloat16 [32, 16, 3, 3, 3], replicated, may hold values from -0.3125 to 0.3125
Outputs:
- first_kernel: float32 [32, 4, 3, 3, 3], P('groups'), parts along dimension 0
- first_bias: float32 [32], P('groups'), parts along dimension 0
- deep_kernel: float32 [64, 16, 3, 3, 3], P('groups'), parts along dimension 0
- deep_bias: float32 [64], P('groups'), parts along dimension 0
There are 2 independent parts, one for each index of `groups`. A program takes and returns all parts, laid end to end along the dimension named above; an argument that names none is the same for every part. Nothing has to cross between parts.
All inputs are finite; a program needn't handle non-finite values.
Results may differ from a plain program's by a relative error of at most 0.0031.
Values may be sent and summed in bfloat16 or wider, within the bound.
A program may use at most 128 MiB of HBM per device.

v0:
```python
import jax
import jax.numpy as jnp
from jax import lax
from jax.sharding import PartitionSpec as P

SLOPE = 0.3


def padded_2(block, sides, width):
    for axis, dim in sides:
        count = lax.axis_size(axis)
        forward = [(i, i + 1) for i in range(count - 1)]
        backward = [(target, source) for source, target in forward]
        low = lax.ppermute(
            lax.slice_in_dim(block, block.shape[dim] - width, None, axis=dim), axis, forward
        )
        high = lax.ppermute(lax.slice_in_dim(block, 0, width, axis=dim), axis, backward)
        block = jnp.concatenate([low, block, high], axis=dim)
    return block


def from_behind(value, axis, steps):
    count = lax.axis_size(axis)
    leading, last = (max(0, -steps), min(count, count - steps))
    return lax.ppermute(value, axis, [(source, source + steps) for source in range(leading, last)])


def leaky(values):
    return jnp.where(values > 0, values, SLOPE * values)


def slope_at(values):
    return jnp.where(values > 0, 1.0, SLOPE)


def deep_gradient(pooled_grad, pre_deep):
    samples, chans, quarter, flat = pooled_grad.shape
    half_depth, half_height, half_width = (pre_deep.shape[2], pre_deep.shape[3], pre_deep.shape[4])
    coarse = (
        pooled_grad.astype(jnp.float32).reshape(
            samples, chans, quarter, 1, half_height // 2, 1, half_width // 2, 1
        )
        / 8.0
    )
    spread = jnp.broadcast_to(
        coarse, (samples, chans, quarter, 2, half_height // 2, 2, half_width // 2, 2)
    )
    spread = spread.reshape(samples, chans, half_depth, half_height, half_width)
    return (spread * slope_at(pre_deep.astype(jnp.float32))).astype(jnp.bfloat16)


def deep_weight_grad(local_grad, padded):
    samples, chans = (padded.shape[0], padded.shape[1])
    coarse_depth, coarse_height, coarse_width = (
        local_grad.shape[2],
        local_grad.shape[3],
        local_grad.shape[4],
    )
    grown = jnp.pad(padded, ((0, 0), (0, 0), (0, 1), (0, 1), (0, 1)))
    phases = grown.reshape(
        samples, chans, coarse_depth + 1, 2, coarse_height + 1, 2, coarse_width + 1, 2
    )
    phases = phases.transpose(0, 1, 3, 5, 7, 2, 4, 6)
    kernels = []
    for depth_tap in range(3):
        for height_tap in range(3):
            for width_tap in range(3):
                depth_off, height_off, width_off = (depth_tap // 2, height_tap // 2, width_tap // 2)
                view = phases[
                    :,
                    :,
                    depth_tap % 2,
                    height_tap % 2,
                    width_tap % 2,
                    depth_off : depth_off + coarse_depth,
                    height_off : height_off + coarse_height,
                    width_off : width_off + coarse_width,
                ]
                kernels.append(
                    jnp.einsum(
                        "sodhw,sidhw->oi", local_grad, view, preferred_element_type=jnp.float32
                    )
                )
    kernel = jnp.stack(kernels, axis=-1).reshape(local_grad.shape[1], chans, 3, 3, 3)
    return (kernel, jnp.sum(local_grad, axis=(0, 2, 3, 4), dtype=jnp.float32))


def transpose_conv(extended, deep_weight):
    samples = extended.shape[0]
    coarse_depth, coarse_height, coarse_width = (
        extended.shape[2] - 1,
        extended.shape[3] - 1,
        extended.shape[4] - 1,
    )
    out_chans = deep_weight.shape[1]
    phase_taps = (((1, 0),), ((2, 0), (0, 1)))
    phases = []
    for depth_phase in range(2):
        for height_phase in range(2):
            for width_phase in range(2):
                views = []
                mats = []
                for depth_tap, depth_step in phase_taps[depth_phase]:
                    for height_tap, height_step in phase_taps[height_phase]:
                        for width_tap, width_step in phase_taps[width_phase]:
                            views.append(
                                extended[
                                    :,
                                    :,
                                    depth_step : depth_step + coarse_depth,
                                    height_step : height_step + coarse_height,
                                    width_step : width_step + coarse_width,
                                ]
                            )
                            mats.append(deep_weight[:, :, depth_tap, height_tap, width_tap])
                stacked = jnp.concatenate(views, axis=1)
                matrix = jnp.concatenate(mats, axis=0)
                phases.append(
                    jnp.einsum(
                        "sodhw,oi->sidhw", stacked, matrix, preferred_element_type=jnp.float32
                    )
                )
    grid = jnp.stack(phases, axis=0).reshape(
        2, 2, 2, samples, out_chans, coarse_depth, coarse_height, coarse_width
    )
    woven = grid.transpose(3, 4, 5, 0, 6, 1, 7, 2).reshape(
        samples, out_chans, 2 * coarse_depth, 2 * coarse_height, 2 * coarse_width
    )
    return woven.astype(jnp.bfloat16)


def first_weight_grad(first_grad, framed):
    chans = framed.shape[1]
    cells_depth, cells_height, cells_width = (
        first_grad.shape[2],
        first_grad.shape[3],
        first_grad.shape[4],
    )
    kernels = []
    for depth_tap in range(3):
        for height_tap in range(3):
            for width_tap in range(3):
                view = framed[
                    :,
                    :,
                    depth_tap : depth_tap + cells_depth,
                    height_tap : height_tap + cells_height,
                    width_tap : width_tap + cells_width,
                ]
                kernels.append(
                    jnp.einsum(
                        "sodhw,sidhw->oi", first_grad, view, preferred_element_type=jnp.float32
                    )
                )
    kernel = jnp.stack(kernels, axis=-1).reshape(first_grad.shape[1], chans, 3, 3, 3)
    return (kernel, jnp.sum(first_grad, axis=(0, 2, 3, 4), dtype=jnp.float32))


def on_device(images, pre_hidden, pre_deep, pooled_grad, deep_weight):
    deep_grad = deep_gradient(pooled_grad, pre_deep)
    hidden = leaky(pre_hidden.astype(jnp.float32)).astype(jnp.bfloat16)
    bordered = padded_2(images, (("depth", 2), ("height", 3)), 1)
    framed = jnp.pad(bordered, ((0, 0), (0, 0), (0, 0), (0, 0), (1, 1)))
    gathered = lax.all_to_all(hidden, "height", split_axis=0, concat_axis=3, tiled=True)
    below = from_behind(gathered[:, :, -1:], "depth", 1)
    padded = jnp.pad(
        jnp.concatenate([below, gathered], axis=2), ((0, 0), (0, 0), (0, 0), (1, 0), (1, 0))
    )
    above = from_behind(deep_grad[:, :, :1], "depth", -1)
    extended = jnp.pad(
        jnp.concatenate([deep_grad, above], axis=2), ((0, 0), (0, 0), (0, 0), (0, 1), (0, 1))
    )
    returned = transpose_conv(extended, deep_weight)
    hidden_grad = lax.all_to_all(returned, "height", split_axis=3, concat_axis=0, tiled=True)
    deep_kernel, deep_bias = deep_weight_grad(deep_grad, padded)
    first_grad = (
        hidden_grad.astype(jnp.float32) * slope_at(pre_hidden.astype(jnp.float32))
    ).astype(jnp.bfloat16)
    first_kernel, first_bias = first_weight_grad(first_grad, framed)
    first_kernel, first_bias, deep_kernel, deep_bias = lax.psum(
        (first_kernel, first_bias, deep_kernel, deep_bias), ("depth", "height")
    )
    return (first_kernel, first_bias, deep_kernel, deep_bias)


def solution(mesh):
    return jax.shard_map(
        on_device,
        mesh=mesh,
        in_specs=(
            P("groups", None, "depth", "height", None),
            P("groups", None, "depth", "height", None),
            P(("groups", "height"), None, "depth", None, None),
            P(("groups", "height"), None, "depth", None),
            P(),
        ),
        out_specs=(
            P("groups", None, None, None, None),
            P("groups"),
            P("groups", None, None, None, None),
            P("groups"),
        ),
        check_vma=False,
    )
```

profile of v0, /device:TPU:0, one launch (start us, length us, event | category | flops | bytes accessed | tf_op | source)
XLA Modules:
  0.0 230.6 jit_solution(8759666628445355263)
XLA Ops:
  2.5 1.3 collective-permute-start.2
  3.8 6.1 %collective-permute-start.1 = (bf16[2,4,1,8,256]{4,1,0,3,2:T(4,128)(2,1)}, bf16[2,4,1,8,256]{4,1,0,3,2:T(4,128)(2,1)}, u32[]{:S(2)}, u32[]{:S(2)}) collective-permute-start(bf16[2,4,1,8,256]{4,1,0,3,2:T(4,128)(2,1)} %get-tuple-element.24), channel_id=1, source_target_pairs={{0,2},{2,4},{4,6},{6,8},{8,10},{10,12},{12,14},{1,3},{3,5},{5,7},{... | collective-permute-start | bytes 98312 | tf_op jit(solution)/shard_map/ppermute | solution.py:14
  13.2 1.3 collective-permute-start
  21.0 2.1 collective-permute-start.3
  28.2 14.3 %copy.88 = bf16[2,2,2,1,16,4,8,128]{4,2,7,1,6,0,5,3:T(2,128)(2,1)} copy(bf16[2,2,2,1,16,4,8,128]{7,4,6,5,2,1,0,3:T(8,128)(2,1)S(1)} %bitcast.783) | data formatting | bytes 2097152 | tf_op jit(solution)/shard_map/convert_element_type | solution.py:129
  42.5 6.9 %copy.89 = bf16[1,16,8,16,256]{4,2,1,0,3:T(8,128)(2,1)S(1)} copy(bf16[1,16,8,16,256]{1,4,3,2,0:T(8,128)(2,1)} %bitcast.752) | data formatting | bytes 2097152 | tf_op jit(solution)/shard_map/convert_element_type | solution.py:129
  49.4 5.9 %all_to_all.27 = bf16[1,16,8,16,256]{4,2,1,0,3:T(8,128)(2,1)S(1)} all-to-all(bf16[1,16,8,16,256]{4,2,1,0,3:T(8,128)(2,1)S(1)} %copy.89), channel_id=1, replica_groups=mesh['groups'=2,'depth'=8,'height'=2] {'height'}, dimensions={3} | all-to-all | bytes 2097152 | tf_op jit(solution)/shard_map/all_to_all | solution.py:174
  55.3 1.3 convert_reduce_fusion
  56.8 4.7 %all_to_all.28 = bf16[2,16,8,8,256]{4,3,2,1,0:T(8,128)(2,1)S(1)} all-to-all(bf16[2,16,8,8,256]{4,3,2,1,0:T(8,128)(2,1)S(1)} %copy.125), channel_id=1, replica_groups=mesh['groups'=2,'depth'=8,'height'=2] {'height'}, dimensions={0} | all-to-all | bytes 2097152 | tf_op jit(solution)/shard_map/all_to_all | solution.py:164
  61.6 4.9 %collective-permute-start.5 = (bf16[1,16,1,16,256]{4,3,2,1,0:T(8,128)(2,1)S(1)}, bf16[1,16,1,16,256]{4,3,2,1,0:T(8,128)(2,1)S(1)}, u32[]{:S(2)}, u32[]{:S(2)}) collective-permute-start(bf16[1,16,1,16,256]{4,3,2,1,0:T(8,128)(2,1)S(1)} %slice.448), channel_id=1, source_target_pairs={{0,2},{2,4},{4,6},{6,8},{8,10},{10,12},{12,14},{1,3},{3,5},{5,7},{... | collective-permute-start | bytes 393224 | tf_op jit(solution)/shard_map/ppermute | solution.py:25
  66.5 1.4 select_maximum_fusion
  68.7 1.6 fusion.81
  72.0 1.6 fusion.78
  75.2 1.6 fusion.75
  78.5 1.6 fusion.72
  84.4 1.8 fusion.66
  87.9 1.6 fusion.63
  91.1 1.6 fusion.60
  94.4 1.6 fusion.57
  97.0 6.6 %copy.193 = bf16[1,16,9,16,256]{1,4,3,2,0:T(8,128)(2,1)} copy(bf16[1,16,9,16,256]{4,3,2,1,0:T(8,128)(2,1)S(1)} %pad_maximum_fusion.4) | data formatting | bytes 2359296
  103.6 10.9 %pad.82 = bf16[1,16,10,18,258]{1,4,3,2,0:T(8,128)(2,1)} pad(bf16[1,16,9,16,256]{1,4,3,2,0:T(8,128)(2,1)} %copy.193, bf16[]{:T(256)} %constant.3.clone.1), padding=0_0x0_0x0_1x1_1x1_1 | pad | bytes 2665730 | tf_op jit(solution)/shard_map/jit(_pad)/pad | solution.py:59
  114.5 24.0 %reshape.237 = bf16[1,16,5,2,9,2,129,2]{1,7,6,5,4,3,2,0:T(2,128)(2,1)} reshape(bf16[1,16,10,18,258]{1,4,3,2,0:T(8,128)(2,1)} %pad.82) | data formatting | bytes 2972160 | tf_op jit(solution)/shard_map/reshape | solution.py:60
  138.5 22.6 %copy.128 = bf16[1,16,5,2,9,2,129,2]{6,1,4,2,7,5,3,0:T(8,128)(2,1)S(1)} copy(bf16[1,16,5,2,9,2,129,2]{1,7,6,5,4,3,2,0:T(2,128)(2,1)} %reshape.237) | data formatting | bytes 2972160 | tf_op jit(solution)/shard_map/reshape | solution.py:60
  166.9 63.7 %all-reduce.4 = (f32[16,4,3,3,3]{0,1,4,3,2:T(4,128)}, f32[16]{0:T(128)}, f32[32,16,3,3,3]{0,1,4,3,2:T(8,128)}, f32[32]{0:T(128)}) all-reduce(f32[16,4,3,3,3]{0,1,4,3,2:T(4,128)S(1)} %bitcast.786, f32[16]{0:T(128)S(1)} %get-tuple-element.10, ...), channel_id=1, replica_groups=mesh['groups'=2,'depth'=8,'height'=2] {'depth','height'}, use_global_device_ids=true, to_apply=%region_0.1 | all-reduce | flops 15600 | bytes 124800 | tf_op jit(solution)/shard_map/psum | solution.py:180
  (143 shorter events, 38.5 us)
Async XLA Ops:
  1.8 8.1 %copy-start.4 = (bf16[2,4,8,8,256]{4,1,0,3,2:T(4,128)(2,1)}, bf16[2,4,8,8,256]{4,1,0,3,2:T(4,128)(2,1)S(1)}, u32[]{:S(2)}) copy-start(bf16[2,4,8,8,256]{4,1,0,3,2:T(4,128)(2,1)S(1)} %copy.92) | copy-start | bytes 786436
  2.5 16.9 %collective-permute-start.2 = (bf16[2,4,1,8,256]{4,1,0,3,2:T(4,128)(2,1)}, bf16[2,4,1,8,256]{4,1,0,3,2:T(4,128)(2,1)}, u32[]{:S(2)}, u32[]{:S(2)}) collective-permute-start(bf16[2,4,1,8,256]{4,1,0,3,2:T(4,128)(2,1)} %get-tuple-element.23), channel_id=1, source_target_pairs={{2,0},{4,2},{6,4},{8,6},{10,8},{12,10},{14,12},{3,1},{5,3},{7,5},{... | collective-permute-start | bytes 98312 | tf_op jit(solution)/shard_map/ppermute | solution.py:17
  3.8 13.7 %collective-permute-start.1 = (bf16[2,4,1,8,256]{4,1,0,3,2:T(4,128)(2,1)}, bf16[2,4,1,8,256]{4,1,0,3,2:T(4,128)(2,1)}, u32[]{:S(2)}, u32[]{:S(2)}) collective-permute-start(bf16[2,4,1,8,256]{4,1,0,3,2:T(4,128)(2,1)} %get-tuple-element.24), channel_id=1, source_target_pairs={{0,2},{2,4},{4,6},{6,8},{8,10},{10,12},{12,14},{1,3},{3,5},{5,7},{... | collective-permute-start | bytes 98312 | tf_op jit(solution)/shard_map/ppermute | solution.py:14
  10.9 1.5 copy-start.6
  11.8 2.7 %copy-start.7 = (bf16[32,16,3,3,3]{0,1,4,3,2:T(8,128)(2,1)S(1)}, bf16[32,16,3,3,3]{0,1,4,3,2:T(8,128)(2,1)}, u32[]{:S(2)}) copy-start(bf16[32,16,3,3,3]{0,1,4,3,2:T(8,128)(2,1)} %param.9) | copy-start | bytes 82948
  13.2 11.2 %collective-permute-start = (bf16[1,32,1,8,128]{4,1,3,2,0:T(8,128)(2,1)S(1)}, bf16[1,32,1,8,128]{4,1,3,2,0:T(8,128)(2,1)S(1)}, u32[]{:S(2)}, u32[]{:S(2)}) collective-permute-start(bf16[1,32,1,8,128]{4,1,3,2,0:T(8,128)(2,1)S(1)} %slice.415), channel_id=1, source_target_pairs={{2,0},{4,2},{6,4},{8,6},{10,8},{12,10},{14,12},{3,1},{5,3},{7,5},{... | collective-permute-start | bytes 196616 | tf_op jit(solution)/shard_map/ppermute | solution.py:25
  20.2 4.9 %copy-start.2 = (bf16[2,4,10,8,256]{4,1,0,3,2:T(4,128)(2,1)}, bf16[2,4,10,8,256]{4,1,0,3,2:T(4,128)(2,1)S(1)}, u32[]{:S(2)}) copy-start(bf16[2,4,10,8,256]{4,1,0,3,2:T(4,128)(2,1)S(1)} %constant_dynamic-update-slice_fusion.7) | copy-start | bytes 983044
  21.0 45.5 %collective-permute-start.3 = (bf16[2,4,10,1,256]{4,1,0,3,2:T(4,128)(2,1)}, bf16[2,4,10,1,256]{4,1,0,3,2:T(4,128)(2,1)}, u32[]{:S(2)}, u32[]{:S(2)}) collective-permute-start(bf16[2,4,10,1,256]{4,1,0,3,2:T(4,128)(2,1)} %get-tuple-element.21), channel_id=1, source_target_pairs={{0,1},{2,3},{4,5},{6,7},{8,9},{10,11},{12,13},{14,15},{16,17},{18,... | collective-permute-start | bytes 122888 | tf_op jit(solution)/shard_map/ppermute | solution.py:14
  23.0 43.5 %collective-permute-start.4 = (bf16[2,4,10,1,256]{4,1,0,3,2:T(4,128)(2,1)}, bf16[2,4,10,1,256]{4,1,0,3,2:T(4,128)(2,1)}, u32[]{:S(2)}, u32[]{:S(2)}) collective-permute-start(bf16[2,4,10,1,256]{4,1,0,3,2:T(4,128)(2,1)} %get-tuple-element.22), channel_id=1, source_target_pairs={{1,0},{3,2},{5,4},{7,6},{9,8},{11,10},{13,12},{15,14},{17,16},{19,... | collective-permute-start | bytes 122888 | tf_op jit(solution)/shard_map/ppermute | solution.py:17
  24.8 0.9 copy-start.12
  24.8 0.9 copy-start.13
  24.9 1.1 copy-start.10
  24.9 1.1 copy-start.11
  25.1 1.2 copy-start.8
  25.2 1.2 copy-start.9
  25.2 1.2 copy-start.24
  25.2 1.2 copy-start.25
  26.0 0.7 copy-start.22
  49.4 5.9 %copy-start = (bf16[2,16,8,8,256]{4,3,2,1,0:T(8,128)(2,1)S(1)}, bf16[2,16,8,8,256]{4,3,2,1,0:T(8,128)(2,1)}, u32[]{:S(2)}) copy-start(bf16[2,16,8,8,256]{4,3,2,1,0:T(8,128)(2,1)} %param.6) | copy-start | bytes 3145732
  56.8 9.7 %copy-start.3 = (bf16[2,4,10,8,256]{4,1,0,3,2:T(4,128)(2,1)S(1)}, bf16[2,4,10,8,256]{4,1,0,3,2:T(4,128)(2,1)}, u32[]{:S(2)}) copy-start(bf16[2,4,10,8,256]{4,1,0,3,2:T(4,128)(2,1)} %copy-done.2) | copy-start | bytes 983044
  61.6 35.3 %collective-permute-start.5 = (bf16[1,16,1,16,256]{4,3,2,1,0:T(8,128)(2,1)S(1)}, bf16[1,16,1,16,256]{4,3,2,1,0:T(8,128)(2,1)S(1)}, u32[]{:S(2)}, u32[]{:S(2)}) collective-permute-start(bf16[1,16,1,16,256]{4,3,2,1,0:T(8,128)(2,1)S(1)} %slice.448), channel_id=1, source_target_pairs={{0,2},{2,4},{4,6},{6,8},{8,10},{10,12},{12,14},{1,3},{3,5},{5,7},{... | collective-permute-start | bytes 393224 | tf_op jit(solution)/shard_map/ppermute | solution.py:25
  70.3 1.7 copy-start.5
  80.1 1.7 copy-start.1
  164.7 2.2 copy-start.26
  (9 other events, 6.2 us)
where the time goes:
time: 233 us; the launch traced here: 231 us
  local copies, waits for them, and re-layouts  95.9 us (41%)
  blocking collectives  74.3 us (32%)
  matrix products  37.7 us (16%)
  starting transfers between devices  16.9 us (7%)
  other arithmetic  4.49 us (2%)
    psum x1, blocking collectives, on_device(): lax.psum((first_kernel, first_bias, deep_kernel, deep_bias), ('depth', 'h...  63.7 us
    reshape x2, local copies, waits for them, and re-layouts, deep_weight_grad(): grown.reshape(samples, chans, coarse_depth + 1, 2, coarse_height + 1, 2,...  46.6 us
    dot_general x27, matrix products, first_weight_grad(): jnp.einsum('sodhw,sidhw->oi', first_grad, view, preferred_element_type=jn...  29 us
    convert_element_type x2, local copies, waits for them, and re-layouts, transpose_conv(): return woven.astype(jnp.bfloat16)  21.2 us
    pad x1, local copies, waits for them, and re-layouts, deep_weight_grad(): grown = jnp.pad(padded, ((0, 0), (0, 0), (0, 1), (0, 1), (0, 1)))  10.9 us
    unnamed x64, local copies, waits for them, and re-layouts  10.4 us
    ppermute x2, starting transfers between devices, padded_2(): lax.ppermute(lax.slice_in_dim(block, block.shape[dim] - width, None, axis...  8.18 us
    ppermute x2, starting transfers between devices, from_behind(): lax.ppermute(value, axis, [(source, source + steps) for source in range(l...  6.15 us
  transfers between devices with their start and end apart: 6, of which 0 were waited for; matrix products, arithmetic and copies ran while one was open for 29% of the time, Pallas kernels for 0%

commit v1 on v0

--- a/solution.py
+++ b/solution.py
@@ -171,7 +171,11 @@
         jnp.concatenate([deep_grad, above], axis=2), ((0, 0), (0, 0), (0, 0), (0, 1), (0, 1))
     )
     returned = transpose_conv(extended, deep_weight)
-    hidden_grad = lax.all_to_all(returned, "height", split_axis=3, concat_axis=0, tiled=True)
+    tile_out = lax.axis_size("height")
+    then = jnp.split(returned, tile_out, axis=3)
+    t1 = jnp.stack(then)
+    new = lax.all_to_all(t1, axis_name="height", split_axis=0, concat_axis=0)
+    hidden_grad = jnp.concatenate(new, axis=0)
     deep_kernel, deep_bias = deep_weight_grad(deep_grad, padded)
     first_grad = (
         hidden_grad.astype(jnp.float32) * slope_at(pre_hidden.astype(jnp.float32))

time: 233 us -> 239 us (1.026)
  local copies, waits for them, and re-layouts: 95.9 us -> 102 us
    another operation x0 -> x3, local copies, waits for them, and re-layouts: none -> 13.3 us  [on_device(): t1 = jnp.stack(then)]
    convert_element_type x2 -> x1, local copies, waits for them, and re-layouts: 21.2 us -> 14.3 us  [transpose_conv(): return woven.astype(jnp.bfloat16)]
  transfers between devices with their start and end apart: 6 -> 6, of which waited for: 0 -> 0; matrix products, arithmetic and copies ran while one was open for 29% -> 30% of each run, Pallas kernels for 0% -> 0%
where the time goes in v1:
time: 239 us; the launch traced here: 237 us
  local copies, waits for them, and re-layouts  102 us (43%)
  blocking collectives  74.3 us (31%)
  matrix products  37.7 us (16%)
  starting transfers between devices  16.9 us (7%)
  other arithmetic  4.23 us (2%)
    psum x1, blocking collectives, on_device(): lax.psum((first_kernel, first_bias, deep_kernel, deep_bias), ('depth', 'h...  63.7 us
    reshape x2, local copies, waits for them, and re-layouts, deep_weight_grad(): grown.reshape(samples, chans, coarse_depth + 1, 2, coarse_height + 1, 2,...  46.7 us
    dot_general x27, matrix products, first_weight_grad(): jnp.einsum('sodhw,sidhw->oi', first_grad, view, preferred_element_type=jn...  29 us
    convert_element_type x1, local copies, waits for them, and re-layouts, transpose_conv(): return woven.astype(jnp.bfloat16)  14.3 us
    another operation x3, local copies, waits for them, and re-layouts, on_device(): t1 = jnp.stack(then)  13.3 us
    pad x1, local copies, waits for them, and re-layouts, deep_weight_grad(): grown = jnp.pad(padded, ((0, 0), (0, 0), (0, 1), (0, 1), (0, 1)))  11 us
    unnamed x64, local copies, waits for them, and re-layouts  10.5 us
    ppermute x2, starting transfers between devices, padded_2(): lax.ppermute(lax.slice_in_dim(block, block.shape[dim] - width, None, axis...  8.17 us
  transfers between devices with their start and end apart: 6, of which 0 were waited for; matrix products, arithmetic and copies ran while one was open for 30% of the time, Pallas kernels for 0%

profile of v1, /device:TPU:0, one launch (start us, length us, event | category | flops | bytes accessed | tf_op | source)
XLA Modules:
  0.0 236.7 jit_solution(16221054289293148030)
XLA Ops:
  2.5 1.3 collective-permute-start.2
  3.8 6.1 %collective-permute-start.1 = (bf16[2,4,1,8,256]{4,1,0,3,2:T(4,128)(2,1)}, bf16[2,4,1,8,256]{4,1,0,3,2:T(4,128)(2,1)}, u32[]{:S(2)}, u32[]{:S(2)}) collective-permute-start(bf16[2,4,1,8,256]{4,1,0,3,2:T(4,128)(2,1)} %get-tuple-element.26), channel_id=1, source_target_pairs={{0,2},{2,4},{4,6},{6,8},{8,10},{10,12},{12,14},{1,3},{3,5},{5,7},{... | collective-permute-start | bytes 98312 | tf_op jit(solution)/shard_map/ppermute | solution.py:14
  20.9 2.1 collective-permute-start.3
  28.1 14.3 %copy.90 = bf16[2,2,2,1,16,4,8,128]{4,2,7,1,6,0,5,3:T(2,128)(2,1)} copy(bf16[2,2,2,1,16,4,8,128]{7,4,6,5,2,1,0,3:T(8,128)(2,1)S(1)} %bitcast.782) | data formatting | bytes 2097152 | tf_op jit(solution)/shard_map/convert_element_type | solution.py:129
  42.4 6.0 %slice_bitcast_fusion.1 = (bf16[1,1,16,8,8,256]{2,5,4,3,1,0:T(8,128)(2,1)}, bf16[1,1,16,8,8,256]{2,5,4,3,1,0:T(8,128)(2,1)}) fusion(bf16[1,16,8,16,256]{1,4,3,2,0:T(8,128)(2,1)} %bitcast.751), kind=kLoop, calls=%fused_computation.1 | loop fusion | bytes 2097152 | tf_op jit(solution)/shard_map/stack | solution.py:176
  48.3 3.7 %copy.91 = bf16[1,1,16,8,8,256]{5,4,3,2,1,0:T(8,128)(2,1)S(1)} copy(bf16[1,1,16,8,8,256]{2,5,4,3,1,0:T(8,128)(2,1)} %get-tuple-element.14) | data formatting | bytes 1048576 | tf_op jit(solution)/shard_map/stack | solution.py:176
  52.0 3.7 %copy.92 = bf16[1,1,16,8,8,256]{5,4,3,2,1,0:T(8,128)(2,1)S(1)} copy(bf16[1,1,16,8,8,256]{2,5,4,3,1,0:T(8,128)(2,1)} %get-tuple-element.15) | data formatting | bytes 1048576 | tf_op jit(solution)/shard_map/stack | solution.py:176
  55.8 5.9 %all_to_all.23 = bf16[2,1,16,8,8,256]{5,4,3,2,1,0:T(8,128)(2,1)S(1)} all-to-all(bf16[2,1,16,8,8,256]{5,4,3,2,1,0:T(8,128)(2,1)S(1)} %pad_maximum_fusion.6), channel_id=1, replica_groups=mesh['groups'=2,'depth'=8,'height'=2] {'height'}, dimensions={0} | all-to-all | bytes 2097152 | tf_op jit(solution)/shard_map/all_to_all | solution.py:177
  62.7 4.7 %all_to_all.24 = bf16[2,16,8,8,256]{4,3,2,1,0:T(8,128)(2,1)S(1)} all-to-all(bf16[2,16,8,8,256]{4,3,2,1,0:T(8,128)(2,1)S(1)} %get-tuple-element.16), channel_id=1, replica_groups=mesh['groups'=2,'depth'=8,'height'=2] {'height'}, dimensions={0} | all-to-all | bytes 2097152 | tf_op jit(solution)/shard_map/all_to_all | solution.py:164
  67.5 4.9 %collective-permute-start.5 = (bf16[1,16,1,16,256]{4,3,2,1,0:T(8,128)(2,1)S(1)}, bf16[1,16,1,16,256]{4,3,2,1,0:T(8,128)(2,1)S(1)}, u32[]{:S(2)}, u32[]{:S(2)}) collective-permute-start(bf16[1,16,1,16,256]{4,3,2,1,0:T(8,128)(2,1)S(1)} %slice.448), channel_id=1, source_target_pairs={{0,2},{2,4},{4,6},{6,8},{8,10},{10,12},{12,14},{1,3},{3,5},{5,7},{... | collective-permute-start | bytes 393224 | tf_op jit(solution)/shard_map/ppermute | solution.py:25
  72.5 1.4 select_maximum_fusion
  74.6 1.6 fusion.81
  77.9 1.6 fusion.78
  81.2 1.6 fusion.75
  84.5 1.6 fusion.72
  90.3 1.8 fusion.66
  93.8 1.6 fusion.63
  97.1 1.6 fusion.60
  100.4 1.6 fusion.57
  102.9 6.7 %copy.193 = bf16[1,16,9,16,256]{1,4,3,2,0:T(8,128)(2,1)} copy(bf16[1,16,9,16,256]{4,3,2,1,0:T(8,128)(2,1)S(1)} %pad_maximum_fusion.4) | data formatting | bytes 2359296
  109.6 11.0 %pad.84 = bf16[1,16,10,18,258]{1,4,3,2,0:T(8,128)(2,1)} pad(bf16[1,16,9,16,256]{1,4,3,2,0:T(8,128)(2,1)} %copy.193, bf16[]{:T(256)} %constant.3.clone.1), padding=0_0x0_0x0_1x1_1x1_1 | pad | bytes 2665730 | tf_op jit(solution)/shard_map/jit(_pad)/pad | solution.py:59
  120.6 24.0 %reshape.236 = bf16[1,16,5,2,9,2,129,2]{1,7,6,5,4,3,2,0:T(2,128)(2,1)} reshape(bf16[1,16,10,18,258]{1,4,3,2,0:T(8,128)(2,1)} %pad.84) | data formatting | bytes 2972160 | tf_op jit(solution)/shard_map/reshape | solution.py:60
  144.6 22.6 %copy.128 = bf16[1,16,5,2,9,2,129,2]{6,1,4,2,7,5,3,0:T(8,128)(2,1)S(1)} copy(bf16[1,16,5,2,9,2,129,2]{1,7,6,5,4,3,2,0:T(2,128)(2,1)} %reshape.236) | data formatting | bytes 2972160 | tf_op jit(solution)/shard_map/reshape | solution.py:60
  173.0 63.7 %all-reduce.4 = (f32[16,4,3,3,3]{0,1,4,3,2:T(4,128)}, f32[16]{0:T(128)}, f32[32,16,3,3,3]{0,1,4,3,2:T(8,128)}, f32[32]{0:T(128)}) all-reduce(f32[16,4,3,3,3]{0,1,4,3,2:T(4,128)S(1)} %bitcast.785, f32[16]{0:T(128)S(1)} %get-tuple-element.10, ...), channel_id=1, replica_groups=mesh['groups'=2,'depth'=8,'height'=2] {'depth','height'}, use_global_device_ids=true, to_apply=%region_0.1 | all-reduce | flops 15600 | bytes 124800 | tf_op jit(solution)/shard_map/psum | solution.py:184
  (145 shorter events, 40.6 us)
Async XLA Ops:
  1.8 8.1 %copy-start.4 = (bf16[2,4,8,8,256]{4,1,0,3,2:T(4,128)(2,1)}, bf16[2,4,8,8,256]{4,1,0,3,2:T(4,128)(2,1)S(1)}, u32[]{:S(2)}) copy-start(bf16[2,4,8,8,256]{4,1,0,3,2:T(4,128)(2,1)S(1)} %copy.93) | copy-start | bytes 786436
  2.5 16.9 %collective-permute-start.2 = (bf16[2,4,1,8,256]{4,1,0,3,2:T(4,128)(2,1)}, bf16[2,4,1,8,256]{4,1,0,3,2:T(4,128)(2,1)}, u32[]{:S(2)}, u32[]{:S(2)}) collective-permute-start(bf16[2,4,1,8,256]{4,1,0,3,2:T(4,128)(2,1)} %get-tuple-element.25), channel_id=1, source_target_pairs={{2,0},{4,2},{6,4},{8,6},{10,8},{12,10},{14,12},{3,1},{5,3},{7,5},{... | collective-permute-start | bytes 98312 | tf_op jit(solution)/shard_map/ppermute | solution.py:17
  3.8 13.6 %collective-permute-start.1 = (bf16[2,4,1,8,256]{4,1,0,3,2:T(4,128)(2,1)}, bf16[2,4,1,8,256]{4,1,0,3,2:T(4,128)(2,1)}, u32[]{:S(2)}, u32[]{:S(2)}) collective-permute-start(bf16[2,4,1,8,256]{4,1,0,3,2:T(4,128)(2,1)} %get-tuple-element.26), channel_id=1, source_target_pairs={{0,2},{2,4},{4,6},{6,8},{8,10},{10,12},{12,14},{1,3},{3,5},{5,7},{... | collective-permute-start | bytes 98312 | tf_op jit(solution)/shard_map/ppermute | solution.py:14
  10.8 1.5 copy-start.6
  11.8 2.7 %copy-start.7 = (bf16[32,16,3,3,3]{0,1,4,3,2:T(8,128)(2,1)S(1)}, bf16[32,16,3,3,3]{0,1,4,3,2:T(8,128)(2,1)}, u32[]{:S(2)}) copy-start(bf16[32,16,3,3,3]{0,1,4,3,2:T(8,128)(2,1)} %param.9) | copy-start | bytes 82948
  13.2 11.1 %collective-permute-start = (bf16[1,32,1,8,128]{4,1,3,2,0:T(8,128)(2,1)S(1)}, bf16[1,32,1,8,128]{4,1,3,2,0:T(8,128)(2,1)S(1)}, u32[]{:S(2)}, u32[]{:S(2)}) collective-permute-start(bf16[1,32,1,8,128]{4,1,3,2,0:T(8,128)(2,1)S(1)} %slice.415), channel_id=1, source_target_pairs={{2,0},{4,2},{6,4},{8,6},{10,8},{12,10},{14,12},{3,1},{5,3},{7,5},{... | collective-permute-start | bytes 196616 | tf_op jit(solution)/shard_map/ppermute | solution.py:25
  20.2 4.9 %copy-start.2 = (bf16[2,4,10,8,256]{4,1,0,3,2:T(4,128)(2,1)}, bf16[2,4,10,8,256]{4,1,0,3,2:T(4,128)(2,1)S(1)}, u32[]{:S(2)}) copy-start(bf16[2,4,10,8,256]{4,1,0,3,2:T(4,128)(2,1)S(1)} %constant_dynamic-update-slice_fusion.7) | copy-start | bytes 983044
  20.9 51.5 %collective-permute-start.3 = (bf16[2,4,10,1,256]{4,1,0,3,2:T(4,128)(2,1)}, bf16[2,4,10,1,256]{4,1,0,3,2:T(4,128)(2,1)}, u32[]{:S(2)}, u32[]{:S(2)}) collective-permute-start(bf16[2,4,10,1,256]{4,1,0,3,2:T(4,128)(2,1)} %get-tuple-element.23), channel_id=1, source_target_pairs={{0,1},{2,3},{4,5},{6,7},{8,9},{10,11},{12,13},{14,15},{16,17},{18,... | collective-permute-start | bytes 122888 | tf_op jit(solution)/shard_map/ppermute | solution.py:14
  23.0 49.5 %collective-permute-start.4 = (bf16[2,4,10,1,256]{4,1,0,3,2:T(4,128)(2,1)}, bf16[2,4,10,1,256]{4,1,0,3,2:T(4,128)(2,1)}, u32[]{:S(2)}, u32[]{:S(2)}) collective-permute-start(bf16[2,4,10,1,256]{4,1,0,3,2:T(4,128)(2,1)} %get-tuple-element.24), channel_id=1, source_target_pairs={{1,0},{3,2},{5,4},{7,6},{9,8},{11,10},{13,12},{15,14},{17,16},{19,... | collective-permute-start | bytes 122888 | tf_op jit(solution)/shard_map/ppermute | solution.py:17
  24.7 0.9 copy-start.12
  24.7 0.9 copy-start.13
  24.8 1.1 copy-start.10
  24.8 1.1 copy-start.11
  25.1 1.2 copy-start.8
  25.1 1.2 copy-start.9
  25.1 1.2 copy-start.24
  25.1 1.2 copy-start.25
  26.0 0.7 copy-start.22
  55.7 6.1 %copy-start = (bf16[2,16,8,8,256]{4,3,2,1,0:T(8,128)(2,1)S(1)}, bf16[2,16,8,8,256]{4,3,2,1,0:T(8,128)(2,1)}, u32[]{:S(2)}) copy-start(bf16[2,16,8,8,256]{4,3,2,1,0:T(8,128)(2,1)} %param.6) | copy-start | bytes 3145732
  62.7 9.7 %copy-start.3 = (bf16[2,4,10,8,256]{4,1,0,3,2:T(4,128)(2,1)S(1)}, bf16[2,4,10,8,256]{4,1,0,3,2:T(4,128)(2,1)}, u32[]{:S(2)}) copy-start(bf16[2,4,10,8,256]{4,1,0,3,2:T(4,128)(2,1)} %copy-done.2) | copy-start | bytes 983044
  67.5 35.3 %collective-permute-start.5 = (bf16[1,16,1,16,256]{4,3,2,1,0:T(8,128)(2,1)S(1)}, bf16[1,16,1,16,256]{4,3,2,1,0:T(8,128)(2,1)S(1)}, u32[]{:S(2)}, u32[]{:S(2)}) collective-permute-start(bf16[1,16,1,16,256]{4,3,2,1,0:T(8,128)(2,1)S(1)} %slice.448), channel_id=1, source_target_pairs={{0,2},{2,4},{4,6},{6,8},{8,10},{10,12},{12,14},{1,3},{3,5},{5,7},{... | collective-permute-start | bytes 393224 | tf_op jit(solution)/shard_map/ppermute | solution.py:25
  76.2 1.7 copy-start.5
  86.1 1.7 copy-start.1
  170.8 2.2 copy-start.26
  (9 other events, 6.2 us)
